TPU v7x, 32 devices: a whole 2x2x4 slice. The times are simulated.
32 devices in a mesh: basin: 4 (over x, core), tile: 8 (over z, y).
Axes of the slice: x: 2, y: 2, z: 4, core: 2. Of those that a mesh axis runs over, the one named last changes fastest.
Arguments:
- ocean_fields: bfloat16 [128, 24, 24, 256], P(('basin', 'tile')), may hold values from -6 to 6
- slot_tiles: int32 [128], P(('basin', 'tile')), may hold values from -1 to 31, as said below
- side_sources: int32 [128, 4], P(('basin', 'tile')), may hold values from -1 to 31, as said below
- corner_sources: int32 [128, 4], P(('basin', 'tile')), may hold values from -1 to 31, as said below
- side_sends: int32 [32, 8, 2], P(('basin', 'tile')), may hold values from -1 to 15, as said below
- corner_sends: int32 [32, 8, 2], P(('basin', 'tile')), may hold values from -1 to 15, as said below
- depth_kernel: bfloat16 [49, 256], replicated, may hold values from -0.875 to 0.875
- expand_weight: bfloat16 [256, 1024], replicated, may hold values from -0.375 to 0.375
- reduce_weight: bfloat16 [1024, 256], replicated, may hold values from -0.1875 to 0.1875
- field_cotangent: bfloat16 [128, 24, 24, 256], P(('basin', 'tile')), may hold values from -6 to 6
Outputs:
- next_fields: bfloat16 [128, 24, 24, 256], P(('basin', 'tile'))
- field_grad: bfloat16 [128, 24, 24, 256], P(('basin', 'tile'))
- kernel_grad: float32 [49, 256], replicated
- expand_grad: float32 [256, 1024], replicated
- reduce_grad: float32 [1024, 256], replicated
Inputs may be any that keep to these rules, and one draw needn't show every extreme that they name: `slot_tiles`: each ocean position of a basin is named by exactly one slot of that basin's devices and land positions by none; -1 marks an empty slot. In every basin some device has all 4 slots filled. `side_sources`: an entry is -1 where the neighbouring position is land or beyond the band's first or last tile row; otherwise it names the neighbour's edge record that faces the slot, the band closing in longitude. Slots that are empty have -1 everywhere. `corner_sources`: as side_sources, for the diagonal neighbours and the corner that faces the slot. `side_sends`: [device, peer, k] is the own edge record that is the k-th record for that peer of the same basin, or -1; each record sent is read by exactly one entry of the peer's side_sources, and every such entry is sent. No device sends to itself. In every basin some pair of devices uses all 2 positions. `corner_sends`: as side_sends, for the corner records and corner_sources.
All inputs are finite; a program needn't handle non-finite values.
Results may differ from a plain program's by a relative error of at most 0.006.
Values may be sent and summed in bfloat16 or wider, within the bound.
No kernel may reach another device: no remote copies, remote signals or barrier semaphores. Data moves between devices by JAX's collectives and lax.ppermute only.
A program may use at most 128 MiB of HBM per device.

v0:
```python
import math

import jax
import jax.numpy as jnp
from jax import lax
from jax.sharding import PartitionSpec as P

KERNEL = 7
HALO_WIDTH = 3


ln_eps = 1e-06


def gelu_parts(pre_act):
    normal_cdf = 0.5 * (1.0 + jax.scipy.special.erf(pre_act * (1.0 / math.sqrt(2.0))))
    density = jnp.exp(-0.5 * pre_act * pre_act) * (1.0 / math.sqrt(2.0 * math.pi))
    return (pre_act * normal_cdf, normal_cdf + pre_act * density)


def edge_pieces(tile_data):
    rim_size = HALO_WIDTH
    slot_count = tile_data.shape[0]
    side_rows = jnp.stack(
        [
            tile_data[:, :rim_size],
            tile_data[:, -rim_size:],
            jnp.swapaxes(tile_data[:, :, :rim_size], 1, 2),
            jnp.swapaxes(tile_data[:, :, -rim_size:], 1, 2),
        ],
        axis=1,
    )
    corner_rows = jnp.stack(
        [
            tile_data[:, :rim_size, :rim_size],
            tile_data[:, :rim_size, -rim_size:],
            tile_data[:, -rim_size:, :rim_size],
            tile_data[:, -rim_size:, -rim_size:],
        ],
        axis=1,
    )
    return (
        side_rows.reshape((slot_count * 4,) + side_rows.shape[2:]),
        corner_rows.reshape((slot_count * 4,) + corner_rows.shape[2:]),
    )


def pick_rows(lookup, codes):
    flat_codes = codes.reshape(-1)
    chosen = jnp.take(lookup, jnp.clip(flat_codes, 0, lookup.shape[0] - 1), axis=0)
    keep_mask = (flat_codes >= 0).reshape((-1,) + (1,) * (lookup.ndim - 1))
    chosen = jnp.where(keep_mask, chosen, jnp.zeros_like(chosen))
    return chosen.reshape(codes.shape + lookup.shape[1:])


def padded_tiles(tile_data, side_own, corner_own, incoming, side_sources, corner_sources):
    side_all = jnp.concatenate([incoming[0].reshape((-1,) + side_own.shape[1:]), side_own], axis=0)
    corner_all = jnp.concatenate(
        [incoming[1].reshape((-1,) + corner_own.shape[1:]), corner_own], axis=0
    )
    side_halo = pick_rows(side_all, side_sources)
    corner_halo = pick_rows(corner_all, corner_sources)
    top_band = jnp.concatenate([corner_halo[:, 0], side_halo[:, 0], corner_halo[:, 1]], axis=2)
    middle = jnp.concatenate(
        [jnp.swapaxes(side_halo[:, 2], 1, 2), tile_data, jnp.swapaxes(side_halo[:, 3], 1, 2)],
        axis=2,
    )
    bottom_band = jnp.concatenate([corner_halo[:, 2], side_halo[:, 1], corner_halo[:, 3]], axis=2)
    return jnp.concatenate([top_band, middle, bottom_band], axis=1)


def depthwise(padded, kernel, out_edge):
    summed = jnp.zeros((padded.shape[0], out_edge, out_edge, padded.shape[-1]), jnp.float32)
    for row_off in range(KERNEL):
        for col_off in range(KERNEL):
            weight_row = kernel[row_off * KERNEL + col_off].astype(jnp.float32)
            window = padded[:, row_off : row_off + out_edge, col_off : col_off + out_edge]
            summed = summed + window.astype(jnp.float32) * weight_row
    return summed


def on_device(
    ocean_fields,
    slot_tiles,
    side_sources,
    corner_sources,
    side_sends,
    corner_sends,
    depth_kernel,
    expand_weight,
    reduce_weight,
    field_cotangent,
):
    slot_count = ocean_fields.shape[0]
    edge_cells = ocean_fields.shape[1]
    channels = ocean_fields.shape[3]
    peer_count = lax.axis_size("tile")
    live_mask = (slot_tiles >= 0)[:, None, None, None]
    fields = jnp.where(live_mask, ocean_fields, jnp.zeros_like(ocean_fields))
    cotangent = jnp.where(live_mask, field_cotangent, jnp.zeros_like(field_cotangent))
    side_own, corner_own = edge_pieces(fields)
    incoming = (
        lax.all_to_all(
            pick_rows(side_own, side_sends[0]), "tile", split_axis=0, concat_axis=0, tiled=True
        ),
        lax.all_to_all(
            pick_rows(corner_own, corner_sends[0]), "tile", split_axis=0, concat_axis=0, tiled=True
        ),
    )
    padded = padded_tiles(fields, side_own, corner_own, incoming, side_sources, corner_sources)
    mixed = depthwise(padded, depth_kernel, edge_cells)
    cells = slot_count * edge_cells * edge_cells
    mixed_rows = mixed.reshape(cells, channels)
    centre = mixed_rows - jnp.mean(mixed_rows, axis=1, keepdims=True)
    scale_inv = lax.rsqrt(jnp.mean(centre * centre, axis=1, keepdims=True) + ln_eps)
    unit_rows = centre * scale_inv
    normed = unit_rows.astype(jnp.bfloat16)
    pre_act = jnp.dot(normed, expand_weight, preferred_element_type=jnp.float32)
    act_value, act_slope = gelu_parts(pre_act)
    activated = act_value.astype(jnp.bfloat16)
    update = jnp.dot(activated, reduce_weight, preferred_element_type=jnp.float32)
    cot_rows = cotangent.reshape(cells, channels)
    reduce_local = jnp.einsum("rf,rc->fc", activated, cot_rows, preferred_element_type=jnp.float32)
    grad_act = jnp.einsum("rc,fc->rf", cot_rows, reduce_weight, preferred_element_type=jnp.float32)
    grad_pre = (grad_act * act_slope).astype(jnp.bfloat16)
    expand_local = jnp.einsum("rc,rf->cf", normed, grad_pre, preferred_element_type=jnp.float32)
    grad_norm = jnp.einsum("rf,cf->rc", grad_pre, expand_weight, preferred_element_type=jnp.float32)
    grad_mixed = scale_inv * (
        grad_norm
        - jnp.mean(grad_norm, axis=1, keepdims=True)
        - unit_rows * jnp.mean(grad_norm * unit_rows, axis=1, keepdims=True)
    )
    grad_mixed = grad_mixed.astype(jnp.bfloat16).reshape(
        slot_count, edge_cells, edge_cells, channels
    )
    grad_mixed_f = grad_mixed.astype(jnp.float32)
    kernel_terms = []
    for row_off in range(KERNEL):
        for col_off in range(KERNEL):
            window = padded[
                :, row_off : row_off + edge_cells, col_off : col_off + edge_cells
            ].astype(jnp.float32)
            kernel_terms.append(jnp.sum(grad_mixed_f * window, axis=(0, 1, 2)))
    kernel_local = jnp.stack(kernel_terms)
    flipped = depth_kernel.reshape(KERNEL, KERNEL, channels)[::-1, ::-1].reshape(
        KERNEL * KERNEL, channels
    )
    cot_side, cot_corner = edge_pieces(grad_mixed)
    cot_in = (
        lax.all_to_all(
            pick_rows(cot_side, side_sends[0]), "tile", split_axis=0, concat_axis=0, tiled=True
        ),
        lax.all_to_all(
            pick_rows(cot_corner, corner_sends[0]), "tile", split_axis=0, concat_axis=0, tiled=True
        ),
    )
    grad_padded = padded_tiles(
        grad_mixed, cot_side, cot_corner, cot_in, side_sources, corner_sources
    )
    spread = depthwise(grad_padded, flipped, edge_cells)
    next_fields = jnp.where(
        live_mask,
        (fields.astype(jnp.float32) + update.reshape(fields.shape)).astype(jnp.bfloat16),
        jnp.zeros_like(fields),
    )
    field_grad = jnp.where(
        live_mask,
        (cotangent.astype(jnp.float32) + spread).astype(jnp.bfloat16),
        jnp.zeros_like(fields),
    )
    kernel_total, expand_total, reduce_total = lax.psum(
        (kernel_local, expand_local, reduce_local), ("basin", "tile")
    )
    factor = 1.0 / math.sqrt(
        lax.axis_size("basin") * peer_count * slot_count * edge_cells * edge_cells
    )
    return (
        next_fields,
        field_grad,
        kernel_total * factor,
        expand_total * factor,
        reduce_total * factor,
    )


def solution(mesh):
    placed = (
        P(("basin", "tile"), None, None, None),
        P(("basin", "tile")),
        P(("basin", "tile"), None),
        P(("basin", "tile"), None),
        P(("basin", "tile"), None, None),
        P(("basin", "tile"), None, None),
        P(),
        P(),
        P(),
        P(("basin", "tile"), None, None, None),
    )
    return jax.shard_map(
        on_device,
        mesh=mesh,
        in_specs=placed,
        out_specs=(
            P(("basin", "tile"), None, None, None),
            P(("basin", "tile"), None, None, None),
            P(),
            P(),
            P(),
        ),
        check_vma=False,
    )
```

profile of v0, /device:TPU:0, one launch (start us, length us, event | category | flops | bytes accessed | tf_op | source)
XLA Modules:
  0.0 285.7 jit_solution(8269214021903822718)
XLA Ops:
  7.2 0.7 broadcast_clamp_fusion.3
  8.1 0.7 broadcast_compare_fusion.3
  8.8 0.7 broadcast_compare_fusion.4
  9.5 1.6 copy_select_fusion.1
  11.4 0.6 gather_fusion
  12.2 0.7 copy.116
  12.9 7.3 %all-to-all-start = ((bf16[8,2,3,3,256]{4,1,3,2,0:T(2,128)(2,1)}), bf16[8,2,3,3,256]{4,1,3,2,0:T(2,128)(2,1)S(1)}, u32[]{:S(2)}, u32[]{:S(2)}) async-start(bf16[8,2,3,3,256]{4,1,3,2,0:T(2,128)(2,1)} %copy.116), calls=%async_computation | async-start | bytes 147456 | tf_op jit(solution)/shard_map/all_to_all | solution.py:106
  20.4 0.2 slice_bitcast_fusion.1
  21.1 0.7 slice_convert_fusion.48
  21.8 0.7 slice_convert_fusion.47
  22.4 0.6 slice_convert_fusion.46
  23.5 0.6 gather_fusion.2
  24.1 1.0 select_select_fusion.3
  25.1 2.1 all-to-all-done
  27.2 3.9 %all-to-all-start.1 = ((bf16[8,2,3,24,256]{4,3,2,1,0:T(8,128)(2,1)}), bf16[8,2,3,24,256]{4,3,2,1,0:T(8,128)(2,1)S(1)}, u32[]{:S(2)}, u32[]{:S(2)}) async-start(bf16[8,2,3,24,256]{4,3,2,1,0:T(8,128)(2,1)} %bitcast.16), calls=%async_computation.1 | async-start | bytes 1179648 | tf_op jit(solution)/shard_map/all_to_all | solution.py:103
  31.3 0.1 pad_maximum_fusion.8
  31.5 0.6 gather_fusion.1
  32.4 14.1 %all-to-all-done.1 = bf16[8,2,3,24,256]{4,3,2,1,0:T(8,128)(2,1)S(1)} async-done(((bf16[8,2,3,24,256]{4,3,2,1,0:T(8,128)(2,1)}), bf16[8,2,3,24,256]{4,3,2,1,0:T(8,128)(2,1)S(1)}, u32[]{:S(2)}, u32[]{:S(2)}) %all-to-all-start.1) | async-done | bytes 589856 | tf_op jit(solution)/shard_map/all_to_all | solution.py:103
  46.6 0.6 gather_fusion.3
  47.2 0.2 select_select_fusion.2
  47.4 0.2 copy_bitcast_fusion.2
  47.6 0.9 copy-done.5
  48.5 3.3 %maximum_maximum_fusion = (bf16[4,27,30,256]{3,1,2,0:T(8,128)(2,1)S(1)}, bf16[4,27,30,256]{3,1,2,0:T(8,128)(2,1)S(1)}) fusion(bf16[4,24,3,256]{3,1,2,0:T(8,128)(2,1)S(1)} %get-tuple-element.112, bf16[4,24,24,256]{3,1,2,0:T(8,128)(2,1)S(1)} %copy-done.5, bf16[4,24,3,256]{3,1,2,0:T(8,128)(2,1)S(1)} %get-tuple-element.110, ...), kind=kLoop, calls=%fused_computation.246 | loop fusion | flops 19906560 | bytes 5160960 | tf_op jit(solution)/shard_map/concatenate | solution.py:69
  51.8 19.1 %fusion.141 = (f32[4,24,24]{1,2,0:T(8,128)S(1)}, f32[4,24,24,256]{3,1,2,0:T(8,128)S(1)}) fusion(f32[256]{0:T(256)S(1)} %bitcast.466, bf16[4,27,30,256]{3,1,2,0:T(8,128)(2,1)S(1)} %get-tuple-element.88, f32[256]{0:T(256)S(1)} %bitcast.419, f32[256]{0:T(256)S(1)} %bitcast.420, f32[256]{0:T(256)S(1)} %bitcast.421, f32[256]{0:T(256)S(1)} %bitcast.422, ...), kind=kLoop, calls=%fused_computation.458 | loop fusion | flops 90240768 | bytes 53438464 | tf_op jit(solution)/shard_map/reduce_sum | solution.py:114
  70.9 2.1 copy.133
  73.1 0.7 multiply_reduce_fusion.1
  74.1 2.6 fusion.130
  76.8 4.0 %multiply_convert_fusion = (bf16[2304,1024]{1,0:T(8,128)(2,1)S(1)}, f32[2304,1024]{1,0:T(8,128)S(1)}) fusion(bf16[2304,256]{1,0:T(8,128)(2,1)S(1)} %fusion.130, bf16[256,1024]{1,0:T(8,128)(2,1)S(1)} %copy-done), kind=kOutput, calls=%fused_computation.65 | convolution fusion | flops 1219756032 | bytes 15859712 | tf_op jit(solution)/shard_map/dot_general | solution.py:118
  80.8 1.5 fusion.147
  82.4 2.2 copy_select_fusion
  84.6 0.2 copy.138
  84.8 2.4 fusion.149
  87.2 4.7 %fusion.5 = bf16[2304,1024]{1,0:T(8,128)(2,1)S(1)} fusion(f32[2304,1024]{1,0:T(8,128)S(1)} %get-tuple-element.222, bf16[2304,256]{1,0:T(8,128)(2,1)S(1)} %bitcast.303, bf16[1024,256]{1,0:T(8,128)(2,1)S(1)} %copy-done.98), kind=kOutput, calls=%fused_computation.64 | convolution fusion | flops 1231552512 | bytes 15859712 | tf_op jit(solution)/shard_map/rc,fc->rf/dot_general | solution.py:124
  91.9 1.7 fusion.140
  93.6 0.4 copy-done.99
  94.1 1.8 multiply_convert_fusion.1
  95.9 1.9 fusion.107
  97.8 2.6 fusion.110
  100.4 7.0 %fusion.100 = (f32[256]{0:T(256)S(1)}, f32[256]{0:T(256)S(1)}, f32[256]{0:T(256)S(1)}, f32[256]{0:T(256)S(1)}, f32[256]{0:T(256)S(1)}, /*index=5*/f32[256]{0:T(2...) fusion(bf16[4,27,30,256]{3,1,2,0:T(8,128)(2,1)S(1)} %copy-done., ...), kind=kLoop, calls=%fused_computation.211 | loop fusion | flops 32435712 | bytes 22431744 | tf_op jit(solution)/shard_map/reduce_sum | solution.py:143
  107.4 7.3 %fusion.128 = (f32[256]{0:T(256)}, f32[256]{0:T(256)}, f32[256]{0:T(256)}, f32[256]{0:T(256)}, f32[256]{0:T(256)}, /*index=5*/f32[256]{0:T(256)}, f32[256]{0:T(2...) fusion(bf16[4,27,30,256]{3,1,2,0:T(8,128)(2,1)S(1)} %get-tuple-, ...), kind=kLoop, calls=%fused_computation.239 | loop fusion | flops 32435712 | bytes 22431744 | tf_op jit(solution)/shard_map/reduce_sum | solution.py:143
  114.7 0.2 copy.146
  115.1 0.6 gather_fusion.4
  115.9 0.7 copy.141
  116.6 3.6 %all-to-all-start.2 = ((bf16[8,2,3,3,256]{4,1,3,2,0:T(2,128)(2,1)}), bf16[8,2,3,3,256]{4,1,3,2,0:T(2,128)(2,1)S(1)}, u32[]{:S(2)}, u32[]{:S(2)}) async-start(bf16[8,2,3,3,256]{4,1,3,2,0:T(2,128)(2,1)} %copy.141), calls=%async_computation.2 | async-start | bytes 147456 | tf_op jit(solution)/shard_map/all_to_all | solution.py:153
  120.4 1.4 gather_fusion.6
  121.8 2.0 select_select_fusion.1
  123.8 3.4 %all-to-all-done.2 = bf16[8,2,3,3,256]{4,1,3,2,0:T(2,128)(2,1)S(1)} async-done(((bf16[8,2,3,3,256]{4,1,3,2,0:T(2,128)(2,1)}), bf16[8,2,3,3,256]{4,1,3,2,0:T(2,128)(2,1)S(1)}, u32[]{:S(2)}, u32[]{:S(2)}) %all-to-all-start.2) | async-done | bytes 73760 | tf_op jit(solution)/shard_map/all_to_all | solution.py:153
  127.2 4.2 %all-to-all-start.3 = ((bf16[8,2,3,24,256]{4,3,2,1,0:T(8,128)(2,1)}), bf16[8,2,3,24,256]{4,3,2,1,0:T(8,128)(2,1)}, u32[]{:S(2)}, u32[]{:S(2)}) async-start(bf16[8,2,3,24,256]{4,3,2,1,0:T(8,128)(2,1)} %bitcast.298), calls=%async_computation.3 | async-start | bytes 1179648 | tf_op jit(solution)/shard_map/all_to_all | solution.py:150
  131.5 4.7 %fusion.148 = f32[256,1024]{1,0:T(8,128)} fusion(bf16[2304,256]{1,0:T(8,128)(2,1)S(1)} %copy-done.9, bf16[2304,1024]{1,0:T(8,128)(2,1)} %copy-done.99), kind=kOutput, calls=%fused_computation.464 | convolution fusion | flops 1207959552 | bytes 6946816 | tf_op jit(solution)/shard_map/rc,rf->cf/dot_general | solution.py:126
  136.5 2.5 copy.160
  139.4 0.2 stack.279
  139.5 41.6 %psum.21 = f32[49,256]{1,0:T(8,128)S(1)} all-reduce(f32[49,256]{1,0:T(8,128)S(1)} %stack.279), channel_id=1, replica_groups=mesh['basin'=4,'tile'=8] {'basin','tile'}, use_global_device_ids=true, to_apply=%region_53.58 | all-reduce | flops 12544 | bytes 100352 | tf_op jit(solution)/shard_map/psum | solution.py:171
  181.2 0.6 broadcast_multiply_fusion.2
  181.9 0.1 pad_maximum_fusion.9
  182.0 0.6 gather_fusion.5
  182.9 1.2 pad_maximum_fusion.5
  184.1 0.6 gather_fusion.7
  184.7 0.2 select_select_fusion
  185.5 3.4 %maximum_maximum_fusion.2 = (bf16[4,27,30,256]{3,1,2,0:T(8,128)(2,1)S(1)}, bf16[4,27,30,256]{3,1,2,0:T(8,128)(2,1)S(1)}) fusion(bf16[4,24,3,256]{3,1,2,0:T(8,128)(2,1)S(1)} %get-tuple-element.108, bf16[4,24,24,256]{3,1,2,0:T(8,128)(2,1)S(1)} %copy.146, bf16[4,24,3,256]{3,1,2,0:T(8,128)(2,1)S(1)} %get-tuple-element.106, ...), kind=kLoop, calls=%fused_computation.248 | loop fusion | flops 19906560 | bytes 5160960 | tf_op jit(solution)/shard_map/concatenate | solution.py:69
  189.3 21.3 %broadcast_select_fusion = bf16[4,24,24,256]{3,1,2,0:T(8,128)(2,1)S(1)} fusion(pred[4]{0:T(512)(128)(4,1)S(1)} %broadcast_compare_fusion.4, f32[256]{0:T(256)S(1)} %bitcast.370, bf16[4,27,30,256]{3,1,2,0:T(8,128)(2,1)S(1)} %get-tuple-element.86, f32[256]{0:T(256)S(1)} %bitcast.371, f32[256]{0:T(256)S(1)} %bitcast.372, f32[256]{0:T(256)S(1)} %bitcast.373, ...), kind=kLoop, calls=%fused_computation.284 | loop fusion | flops 92602368 | bytes 53429252 | tf_op jit(solution)/shard_map/jit(_where)/select_n | solution.py:166
  210.6 1.2 copy.161
  211.9 63.4 %all-reduce.3.cloned.1.call-done = (f32[256,1024]{1,0:T(8,128)}, f32[1024,256]{1,0:T(8,128)}) async-done(((f32[256,1024]{1,0:T(8,128)}, f32[1024,256]{1,0:T(8,128)}), (f32[256,1024]{1,0:T(8,128)}, f32[1024,256]{1,0:T(8,128)})) %all-reduce.3.cloned.1.call-update) | async-done | bytes 2097168 | tf_op jit(solution)/shard_map/psum | solution.py:171
  275.3 2.4 broadcast_multiply_fusion
  277.7 1.1 broadcast_multiply_fusion.1
  (277 shorter events, 4.0 us)
Async XLA Ops:
  7.2 69.6 %copy-start = (bf16[256,1024]{1,0:T(8,128)(2,1)S(1)}, bf16[256,1024]{1,0:T(8,128)(2,1)}, u32[]{:S(2)}) copy-start(bf16[256,1024]{1,0:T(8,128)(2,1)} %param.25) | copy-start | bytes 1572868
  7.2 13.0 %copy-start.15 = (s32[4,4]{1,0:T(4,128)S(1)}, s32[4,4]{1,0:T(4,128)}, u32[]{:S(2)}) copy-start(s32[4,4]{1,0:T(4,128)} %param.21) | copy-start | bytes 196
  9.5 11.1 %copy-start.97 = (s32[1,8,2]{1,2,0:T(2,128)S(1)}, s32[1,8,2]{1,2,0:T(2,128)}, u32[]{:S(2)}) copy-start(s32[1,8,2]{1,2,0:T(2,128)} %param.22) | copy-start | bytes 196
  9.5 11.3 %copy-start.16 = (s32[4,4]{1,0:T(4,128)S(1)}, s32[4,4]{1,0:T(4,128)}, u32[]{:S(2)}) copy-start(s32[4,4]{1,0:T(4,128)} %param.20) | copy-start | bytes 196
  9.5 11.4 %copy-start.14 = (bf16[49,256]{1,0:T(8,128)(2,1)S(1)}, bf16[49,256]{1,0:T(8,128)(2,1)}, u32[]{:S(2)}) copy-start(bf16[49,256]{1,0:T(8,128)(2,1)} %param.24) | copy-start | bytes 75268
  11.0 12.4 %copy-start.4 = (bf16[4,24,24,256]{3,1,2,0:T(8,128)(2,1)}, bf16[4,24,24,256]{3,1,2,0:T(8,128)(2,1)S(1)}, u32[]{:S(2)}) copy-start(bf16[4,24,24,256]{3,1,2,0:T(8,128)(2,1)S(1)} %copy_select_fusion.1) | copy-start | bytes 3538948
  12.9 14.3 %all-to-all-start = ((bf16[8,2,3,3,256]{4,1,3,2,0:T(2,128)(2,1)}), bf16[8,2,3,3,256]{4,1,3,2,0:T(2,128)(2,1)S(1)}, u32[]{:S(2)}, u32[]{:S(2)}) async-start(bf16[8,2,3,3,256]{4,1,3,2,0:T(2,128)(2,1)} %copy.116), calls=%async_computation | async-start | bytes 147456 | tf_op jit(solution)/shard_map/all_to_all | solution.py:106
  20.3 11.8 %copy-start.87 = (pred[16]{0:T(512)(128)(4,1)}, pred[16]{0:T(512)(128)(4,1)S(1)}, u32[]{:S(2)}) copy-start(pred[16]{0:T(512)(128)(4,1)S(1)} %compare_and_fusion.2) | copy-start | bytes 52
  20.8 6.4 %copy-start.89 = (pred[16]{0:T(512)(128)(4,1)}, pred[16]{0:T(512)(128)(4,1)S(1)}, u32[]{:S(2)}) copy-start(pred[16]{0:T(512)(128)(4,1)S(1)} %compare_and_fusion.1) | copy-start | bytes 52
  25.1 22.1 %copy-start.90 = (pred[16]{0:T(512)(128)(4,1)}, pred[16]{0:T(512)(128)(4,1)S(1)}, u32[]{:S(2)}) copy-start(pred[16]{0:T(512)(128)(4,1)S(1)} %compare_and_fusion) | copy-start | bytes 52
  27.2 19.3 %all-to-all-start.1 = ((bf16[8,2,3,24,256]{4,3,2,1,0:T(8,128)(2,1)}), bf16[8,2,3,24,256]{4,3,2,1,0:T(8,128)(2,1)S(1)}, u32[]{:S(2)}, u32[]{:S(2)}) async-start(bf16[8,2,3,24,256]{4,3,2,1,0:T(8,128)(2,1)} %bitcast.16), calls=%async_computation.1 | async-start | bytes 1179648 | tf_op jit(solution)/shard_map/all_to_all | solution.py:103
  31.2 16.0 %copy-start.94 = (pred[16]{0:T(512)(128)(4,1)}, pred[16]{0:T(512)(128)(4,1)S(1)}, u32[]{:S(2)}) copy-start(pred[16]{0:T(512)(128)(4,1)S(1)} %ge.65) | copy-start | bytes 52
  31.3 15.9 %copy-start.92 = (pred[16]{0:T(512)(128)(4,1)}, pred[16]{0:T(512)(128)(4,1)S(1)}, u32[]{:S(2)}) copy-start(pred[16]{0:T(512)(128)(4,1)S(1)} %ge.69) | copy-start | bytes 52
  51.8 19.1 %copy-start.2 = (bf16[4,27,30,256]{3,1,2,0:T(8,128)(2,1)}, bf16[4,27,30,256]{3,1,2,0:T(8,128)(2,1)S(1)}, u32[]{:S(2)}) copy-start(bf16[4,27,30,256]{3,1,2,0:T(8,128)(2,1)S(1)} %get-tuple-element.87) | copy-start | bytes 4976644
  76.7 4.0 %copy-start.8 = (bf16[2304,256]{1,0:T(8,128)(2,1)}, bf16[2304,256]{1,0:T(8,128)(2,1)S(1)}, u32[]{:S(2)}) copy-start(bf16[2304,256]{1,0:T(8,128)(2,1)S(1)} %fusion.130) | copy-start | bytes 3538948
  76.7 4.0 %copy-start.98 = (bf16[1024,256]{1,0:T(8,128)(2,1)S(1)}, bf16[1024,256]{1,0:T(8,128)(2,1)}, u32[]{:S(2)}) copy-start(bf16[1024,256]{1,0:T(8,128)(2,1)} %param.26) | copy-start | bytes 1572868
  87.2 4.7 %copy-start.7 = (f32[4,24,24,256]{3,2,1,0:T(8,128)S(1)}, f32[4,24,24,256]{3,2,1,0:T(8,128)}, u32[]{:S(2)}) copy-start(f32[4,24,24,256]{3,2,1,0:T(8,128)} %copy.133) | copy-start | bytes 7077892
  116.6 10.6 %all-to-all-start.2 = ((bf16[8,2,3,3,256]{4,1,3,2,0:T(2,128)(2,1)}), bf16[8,2,3,3,256]{4,1,3,2,0:T(2,128)(2,1)S(1)}, u32[]{:S(2)}, u32[]{:S(2)}) async-start(bf16[8,2,3,3,256]{4,1,3,2,0:T(2,128)(2,1)} %copy.141), calls=%async_computation.2 | async-start | bytes 147456 | tf_op jit(solution)/shard_map/all_to_all | solution.py:153
  120.3 11.2 %copy-start.9 = (bf16[2304,256]{1,0:T(8,128)(2,1)S(1)}, bf16[2304,256]{1,0:T(8,128)(2,1)}, u32[]{:S(2)}) copy-start(bf16[2304,256]{1,0:T(8,128)(2,1)} %copy-done.8) | copy-start | bytes 3538948
  127.2 55.7 %all-to-all-start.3 = ((bf16[8,2,3,24,256]{4,3,2,1,0:T(8,128)(2,1)}), bf16[8,2,3,24,256]{4,3,2,1,0:T(8,128)(2,1)}, u32[]{:S(2)}, u32[]{:S(2)}) async-start(bf16[8,2,3,24,256]{4,3,2,1,0:T(8,128)(2,1)} %bitcast.298), calls=%async_computation.3 | async-start | bytes 1179648 | tf_op jit(solution)/shard_map/all_to_all | solution.py:150
  131.4 143.9 %all-reduce.3.cloned.1.call-start = ((), (), s32[]{:S(2)}) async-start(), calls=%async_computation.4 | async-start | bytes 4194304 | tf_op jit(solution)/shard_map/psum | solution.py:171
  136.5 46.2 %copy-start.88 = (pred[16]{0:T(512)(128)(4,1)S(1)}, pred[16]{0:T(512)(128)(4,1)}, u32[]{:S(2)}) copy-start(pred[16]{0:T(512)(128)(4,1)} %copy-done.87) | copy-start | bytes 52
  136.5 46.2 %copy-start.95 = (pred[16]{0:T(512)(128)(4,1)S(1)}, pred[16]{0:T(512)(128)(4,1)}, u32[]{:S(2)}) copy-start(pred[16]{0:T(512)(128)(4,1)} %copy-done.94) | copy-start | bytes 52
  185.1 3.8 %copy-start.11 = (bf16[4,24,24,256]{3,2,1,0:T(8,128)(2,1)S(1)}, bf16[4,24,24,256]{3,2,1,0:T(8,128)(2,1)}, u32[]{:S(2)}) copy-start(bf16[4,24,24,256]{3,2,1,0:T(8,128)(2,1)} %param.27) | copy-start | bytes 3538948
  185.1 3.8 %copy-start.48 = (f32[1,256]{1,0:T(1,128)S(1)}, f32[1,256]{1,0:T(1,128)}, u32[]{:S(2)}) copy-start(f32[1,256]{1,0:T(1,128)} %get-tuple-element.121) | copy-start | bytes 3076
  185.1 3.8 %copy-start.49 = (f32[1,256]{1,0:T(1,128)S(1)}, f32[1,256]{1,0:T(1,128)}, u32[]{:S(2)}) copy-start(f32[1,256]{1,0:T(1,128)} %get-tuple-element.122) | copy-start | bytes 3076
  185.1 3.8 %copy-start.50 = (f32[1,256]{1,0:T(1,128)S(1)}, f32[1,256]{1,0:T(1,128)}, u32[]{:S(2)}) copy-start(f32[1,256]{1,0:T(1,128)} %get-tuple-element.123) | copy-start | bytes 3076
  185.1 3.8 %copy-start.51 = (f32[1,256]{1,0:T(1,128)S(1)}, f32[1,256]{1,0:T(1,128)}, u32[]{:S(2)}) copy-start(f32[1,256]{1,0:T(1,128)} %get-tuple-element.124) | copy-start | bytes 3076
  185.2 3.8 %copy-start.52 = (f32[1,256]{1,0:T(1,128)S(1)}, f32[1,256]{1,0:T(1,128)}, u32[]{:S(2)}) copy-start(f32[1,256]{1,0:T(1,128)} %get-tuple-element.125) | copy-start | bytes 3076
  185.2 3.8 %copy-start.53 = (f32[1,256]{1,0:T(1,128)S(1)}, f32[1,256]{1,0:T(1,128)}, u32[]{:S(2)}) copy-start(f32[1,256]{1,0:T(1,128)} %get-tuple-element.126) | copy-start | bytes 3076
  185.2 3.8 %copy-start.54 = (f32[1,256]{1,0:T(1,128)S(1)}, f32[1,256]{1,0:T(1,128)}, u32[]{:S(2)}) copy-start(f32[1,256]{1,0:T(1,128)} %get-tuple-element.127) | copy-start | bytes 3076
  185.2 3.8 %copy-start.55 = (f32[1,256]{1,0:T(1,128)S(1)}, f32[1,256]{1,0:T(1,128)}, u32[]{:S(2)}) copy-start(f32[1,256]{1,0:T(1,128)} %get-tuple-element.128) | copy-start | bytes 3076
  185.2 3.8 %copy-start.56 = (f32[1,256]{1,0:T(1,128)S(1)}, f32[1,256]{1,0:T(1,128)}, u32[]{:S(2)}) copy-start(f32[1,256]{1,0:T(1,128)} %get-tuple-element.129) | copy-start | bytes 3076
  185.2 3.8 %copy-start.57 = (f32[1,256]{1,0:T(1,128)S(1)}, f32[1,256]{1,0:T(1,128)}, u32[]{:S(2)}) copy-start(f32[1,256]{1,0:T(1,128)} %get-tuple-element.130) | copy-start | bytes 3076
  185.2 3.8 %copy-start.58 = (f32[1,256]{1,0:T(1,128)S(1)}, f32[1,256]{1,0:T(1,128)}, u32[]{:S(2)}) copy-start(f32[1,256]{1,0:T(1,128)} %get-tuple-element.131) | copy-start | bytes 3076
  185.2 3.8 %copy-start.59 = (f32[1,256]{1,0:T(1,128)S(1)}, f32[1,256]{1,0:T(1,128)}, u32[]{:S(2)}) copy-start(f32[1,256]{1,0:T(1,128)} %get-tuple-element.132) | copy-start | bytes 3076
  185.2 3.8 %copy-start.60 = (f32[1,256]{1,0:T(1,128)S(1)}, f32[1,256]{1,0:T(1,128)}, u32[]{:S(2)}) copy-start(f32[1,256]{1,0:T(1,128)} %get-tuple-element.133) | copy-start | bytes 3076
  185.2 3.8 %copy-start.61 = (f32[1,256]{1,0:T(1,128)S(1)}, f32[1,256]{1,0:T(1,128)}, u32[]{:S(2)}) copy-start(f32[1,256]{1,0:T(1,128)} %get-tuple-element.134) | copy-start | bytes 3076
  185.3 3.8 %copy-start.62 = (f32[1,256]{1,0:T(1,128)S(1)}, f32[1,256]{1,0:T(1,128)}, u32[]{:S(2)}) copy-start(f32[1,256]{1,0:T(1,128)} %get-tuple-element.135) | copy-start | bytes 3076
  185.3 3.8 %copy-start.63 = (f32[1,256]{1,0:T(1,128)S(1)}, f32[1,256]{1,0:T(1,128)}, u32[]{:S(2)}) copy-start(f32[1,256]{1,0:T(1,128)} %get-tuple-element.136) | copy-start | bytes 3076
  185.3 3.8 %copy-start.64 = (f32[1,256]{1,0:T(1,128)S(1)}, f32[1,256]{1,0:T(1,128)}, u32[]{:S(2)}) copy-start(f32[1,256]{1,0:T(1,128)} %get-tuple-element.137) | copy-start | bytes 3076
  185.3 3.8 %copy-start.65 = (f32[1,256]{1,0:T(1,128)S(1)}, f32[1,256]{1,0:T(1,128)}, u32[]{:S(2)}) copy-start(f32[1,256]{1,0:T(1,128)} %get-tuple-element.138) | copy-start | bytes 3076
  185.3 3.8 %copy-start.66 = (f32[1,256]{1,0:T(1,128)S(1)}, f32[1,256]{1,0:T(1,128)}, u32[]{:S(2)}) copy-start(f32[1,256]{1,0:T(1,128)} %get-tuple-element.139) | copy-start | bytes 3076
  185.3 3.8 %copy-start.67 = (f32[1,256]{1,0:T(1,128)S(1)}, f32[1,256]{1,0:T(1,128)}, u32[]{:S(2)}) copy-start(f32[1,256]{1,0:T(1,128)} %get-tuple-element.140) | copy-start | bytes 3076
  185.3 3.8 %copy-start.68 = (f32[1,256]{1,0:T(1,128)S(1)}, f32[1,256]{1,0:T(1,128)}, u32[]{:S(2)}) copy-start(f32[1,256]{1,0:T(1,128)} %get-tuple-element.141) | copy-start | bytes 3076
  185.3 3.8 %copy-start.69 = (f32[1,256]{1,0:T(1,128)S(1)}, f32[1,256]{1,0:T(1,128)}, u32[]{:S(2)}) copy-start(f32[1,256]{1,0:T(1,128)} %get-tuple-element.142) | copy-start | bytes 3076
  185.3 3.8 %copy-start.70 = (f32[1,256]{1,0:T(1,128)S(1)}, f32[1,256]{1,0:T(1,128)}, u32[]{:S(2)}) copy-start(f32[1,256]{1,0:T(1,128)} %get-tuple-element.143) | copy-start | bytes 3076
  185.3 3.8 %copy-start.71 = (f32[1,256]{1,0:T(1,128)S(1)}, f32[1,256]{1,0:T(1,128)}, u32[]{:S(2)}) copy-start(f32[1,256]{1,0:T(1,128)} %get-tuple-element.144) | copy-start | bytes 3076
  185.4 3.8 %copy-start.72 = (f32[1,256]{1,0:T(1,128)S(1)}, f32[1,256]{1,0:T(1,128)}, u32[]{:S(2)}) copy-start(f32[1,256]{1,0:T(1,128)} %get-tuple-element.145) | copy-start | bytes 3076
  185.4 3.8 %copy-start.73 = (f32[1,256]{1,0:T(1,128)S(1)}, f32[1,256]{1,0:T(1,128)}, u32[]{:S(2)}) copy-start(f32[1,256]{1,0:T(1,128)} %get-tuple-element.146) | copy-start | bytes 3076
  185.4 3.8 %copy-start.74 = (f32[1,256]{1,0:T(1,128)S(1)}, f32[1,256]{1,0:T(1,128)}, u32[]{:S(2)}) copy-start(f32[1,256]{1,0:T(1,128)} %get-tuple-element.147) | copy-start | bytes 3076
  185.4 3.8 %copy-start.75 = (f32[1,256]{1,0:T(1,128)S(1)}, f32[1,256]{1,0:T(1,128)}, u32[]{:S(2)}) copy-start(f32[1,256]{1,0:T(1,128)} %get-tuple-element.148) | copy-start | bytes 3076
  185.4 3.8 %copy-start.76 = (f32[1,256]{1,0:T(1,128)S(1)}, f32[1,256]{1,0:T(1,128)}, u32[]{:S(2)}) copy-start(f32[1,256]{1,0:T(1,128)} %get-tuple-element.149) | copy-start | bytes 3076
  185.4 3.8 %copy-start.77 = (f32[1,256]{1,0:T(1,128)S(1)}, f32[1,256]{1,0:T(1,128)}, u32[]{:S(2)}) copy-start(f32[1,256]{1,0:T(1,128)} %get-tuple-element.150) | copy-start | bytes 3076
  185.4 3.8 %copy-start.78 = (f32[1,256]{1,0:T(1,128)S(1)}, f32[1,256]{1,0:T(1,128)}, u32[]{:S(2)}) copy-start(f32[1,256]{1,0:T(1,128)} %get-tuple-element.151) | copy-start | bytes 3076
  185.4 3.8 %copy-start.79 = (f32[1,256]{1,0:T(1,128)S(1)}, f32[1,256]{1,0:T(1,128)}, u32[]{:S(2)}) copy-start(f32[1,256]{1,0:T(1,128)} %get-tuple-element.152) | copy-start | bytes 3076
  185.4 3.8 %copy-start.80 = (f32[1,256]{1,0:T(1,128)S(1)}, f32[1,256]{1,0:T(1,128)}, u32[]{:S(2)}) copy-start(f32[1,256]{1,0:T(1,128)} %get-tuple-element.153) | copy-start | bytes 3076
  185.4 3.8 %copy-start.81 = (f32[1,256]{1,0:T(1,128)S(1)}, f32[1,256]{1,0:T(1,128)}, u32[]{:S(2)}) copy-start(f32[1,256]{1,0:T(1,128)} %get-tuple-element.154) | copy-start | bytes 3076
  185.5 3.8 %copy-start.82 = (f32[1,256]{1,0:T(1,128)S(1)}, f32[1,256]{1,0:T(1,128)}, u32[]{:S(2)}) copy-start(f32[1,256]{1,0:T(1,128)} %get-tuple-element.155) | copy-start | bytes 3076
  185.5 3.8 %copy-start.83 = (f32[1,256]{1,0:T(1,128)S(1)}, f32[1,256]{1,0:T(1,128)}, u32[]{:S(2)}) copy-start(f32[1,256]{1,0:T(1,128)} %get-tuple-element.156) | copy-start | bytes 3076
  185.5 3.8 %copy-start.84 = (f32[1,256]{1,0:T(1,128)S(1)}, f32[1,256]{1,0:T(1,128)}, u32[]{:S(2)}) copy-start(f32[1,256]{1,0:T(1,128)} %get-tuple-element.157) | copy-start | bytes 3076
  185.5 3.8 %copy-start.85 = (f32[1,256]{1,0:T(1,128)S(1)}, f32[1,256]{1,0:T(1,128)}, u32[]{:S(2)}) copy-start(f32[1,256]{1,0:T(1,128)} %get-tuple-element.158) | copy-start | bytes 3076
  185.5 3.8 %copy-start.86 = (f32[1,256]{1,0:T(1,128)S(1)}, f32[1,256]{1,0:T(1,128)}, u32[]{:S(2)}) copy-start(f32[1,256]{1,0:T(1,128)} %get-tuple-element.159) | copy-start | bytes 3076
  210.6 68.2 %copy-start.1 = (bf16[256,1024]{1,0:T(8,128)(2,1)S(1)}, bf16[256,1024]{1,0:T(8,128)(2,1)}, u32[]{:S(2)}) copy-start(bf16[256,1024]{1,0:T(8,128)(2,1)} %param.25) | copy-start | bytes 1572868
  (41 other events, 108.0 us)
Sparse Core Ops, SparseCore 0:
  139.2 136.1 all-reduce.2
where the time goes:
time: 287 us; the launch traced here: 286 us
  other arithmetic  88.7 us (31%)
  waiting for transfers between devices  83.1 us (29%)
  blocking collectives  41.6 us (14%)
  starting transfers between devices  19.1 us (7%)
  matrix products  19 us (7%)
  local copies, waits for them, and re-layouts  18.1 us (6%)
  between operations  16.1 us (6%)
    psum x1, waiting for transfers between devices, on_device(): lax.psum((kernel_local, expand_local, reduce_local), ('basin', 'tile'))  63.4 us
    psum x1, blocking collectives, on_device(): lax.psum((kernel_local, expand_local, reduce_local), ('basin', 'tile'))  41.6 us
    select_n x1, other arithmetic, on_device(): jnp.where(live_mask, (cotangent.astype(jnp.float32) + spread).astype(jnp....  21.3 us
    reduce_sum x1, other arithmetic, on_device(): centre = mixed_rows - jnp.mean(mixed_rows, axis=1, keepdims=True)  19.1 us
    reduce_sum x4, other arithmetic, on_device(): kernel_terms.append(jnp.sum(grad_mixed_f * window, axis=(0, 1, 2)))  18.8 us
    all_to_all x1, waiting for transfers between devices, on_device(): lax.all_to_all(pick_rows(side_own, side_sends[0]), 'tile', split_axis=0,...  14.1 us
    all_to_all x1, starting transfers between devices, on_device(): lax.all_to_all(pick_rows(corner_own, corner_sends[0]), 'tile', split_axis...  7.31 us
    concatenate x2, other arithmetic, padded_tiles(): return jnp.concatenate([top_band, middle, bottom_band], axis=1)  6.74 us
  transfers between devices with their start and end apart: 5, of which 4 were waited for; matrix products, arithmetic and copies ran while one was open for 16% of the time, Pallas kernels for 0%

commit v1 on v0

v1 whole, which is shorter than its diff:
```python
import functools
import math

import jax
import jax.numpy as jnp
from jax import lax
from jax.experimental import pallas as pl
from jax.experimental.pallas import tpu as pltpu
from jax.sharding import PartitionSpec as P

KERNEL = 7
TAPS = KERNEL * KERNEL
RIM = 3
LANES = 128
COL0 = 8
LN_EPS = 1e-06
F32 = jnp.float32
BF16 = jnp.bfloat16
VMEM_LIMIT = 60 * 1024 * 1024


def mxu(lhs, rhs, lhs_dim, rhs_dim):
    return lax.dot_general(
        lhs, rhs, (((lhs_dim,), (rhs_dim,)), ((), ())), preferred_element_type=F32
    )


def gelu_parts(pre):
    cdf = 0.5 * (1.0 + lax.erf(pre * (1.0 / math.sqrt(2.0))))
    density = jnp.exp(-0.5 * pre * pre) * (1.0 / math.sqrt(2.0 * math.pi))
    return pre * cdf, cdf + pre * density


def live_factor(slot_ref, slot):
    return jnp.where(slot_ref[slot] >= 0, 1.0, 0.0).astype(F32)


def own_records(cells, side, corner, base, edge, slots):
    area = edge * edge
    rim_rows = RIM * edge
    far = edge - RIM
    for grp in range(cells.shape[0]):
        for s in range(slots):
            at = base + 4 * s
            start = s * area
            side[at, grp] = cells[grp, start : start + rim_rows]
            side[at + 1, grp] = cells[grp, start + area - rim_rows : start + area]
            for c in range(RIM):
                rows = slice(c * edge, (c + 1) * edge)
                side[at + 2, grp, rows] = cells[grp, pl.ds(start + c, edge, stride=edge)]
                side[at + 3, grp, rows] = cells[grp, pl.ds(start + far + c, edge, stride=edge)]
            for e in range(4):
                row0 = far if e // 2 else 0
                col0 = far if e % 2 else 0
                for r in range(RIM):
                    first = start + (row0 + r) * edge + col0
                    corner[at + e, grp, RIM * r : RIM * r + RIM] = cells[grp, first : first + RIM]


def send_records(send, side, corner, side_sends, corner_sends, zero_at):
    peers = send.shape[0]
    groups = side.shape[1]
    cap = side_sends.shape[0] // peers

    def one_peer(p, carry):
        for grp in range(groups):
            pieces = []
            for table, sends in ((side, side_sends), (corner, corner_sends)):
                for k in range(cap):
                    code = sends[p * cap + k]
                    pieces.append(table[jnp.where(code < 0, zero_at, code), grp])
            block = jnp.concatenate(pieces, axis=0)
            send[p, :, grp * LANES : (grp + 1) * LANES] = block.astype(BF16)
        return carry

    lax.fori_loop(0, peers, one_peer, 0)


def received_records(recv, side, corner, cap):
    groups = side.shape[1]
    n_side = side.shape[2]
    n_corner = corner.shape[2]

    def one_peer(p, carry):
        for grp in range(groups):
            block = recv[p, :, grp * LANES : (grp + 1) * LANES].astype(F32)
            for k in range(cap):
                side[p * cap + k, grp] = block[k * n_side : (k + 1) * n_side]
                first = cap * n_side + k * n_corner
                corner[p * cap + k, grp] = block[first : first + n_corner]
        return carry

    lax.fori_loop(0, recv.shape[0], one_peer, 0)


def place_rim(padded, side, corner, side_sources, corner_sources, slot, zero_at, edge):
    for e in range(4):
        code = side_sources[slot * 4 + e]
        at = jnp.where(code < 0, zero_at, code)
        for grp in range(side.shape[1]):
            for c in range(RIM):
                piece = side[at, grp, c * edge : (c + 1) * edge]
                if e < 2:
                    row = c if e == 0 else RIM + edge + c
                    padded[grp, row, COL0 : COL0 + edge] = piece
                else:
                    col = COL0 - RIM + c if e == 2 else COL0 + edge + c
                    padded[grp, RIM : RIM + edge, col] = piece
        code = corner_sources[slot * 4 + e]
        at = jnp.where(code < 0, zero_at, code)
        row0 = RIM + edge if e // 2 else 0
        col0 = COL0 + edge if e % 2 else COL0 - RIM
        for grp in range(side.shape[1]):
            for r in range(RIM):
                padded[grp, row0 + r, col0 : col0 + RIM] = corner[
                    at, grp, RIM * r : RIM * r + RIM
                ]


def spread_taps(taps, kernel_ref):
    for grp in range(taps.shape[0]):
        for t in range(TAPS):
            row = kernel_ref[t : t + 1, grp * LANES : (grp + 1) * LANES].astype(F32)
            taps[grp, t] = jnp.broadcast_to(row, taps.shape[2:])


def conv_group(padded, taps, grp, edge, part, flipped, emit):
    blocks = edge // 8
    lane = lax.broadcasted_iota(jnp.int32, (8, LANES), 0)
    for blk in range(blocks):
        acc = [None] * edge
        for b in range(KERNEL):
            west = part == "rim" and blk == 0 and b < RIM
            east = part == "rim" and blk == blocks - 1 and b > RIM
            weights = []
            for a in range(KERNEL):
                t = a * KERNEL + b
                weights.append(taps[grp, TAPS - 1 - t if flipped else t])
            for r in range(edge + 2 * RIM):
                inner = RIM <= r < RIM + edge
                if part == "own" and not inner:
                    continue
                if part == "rim" and inner and not (west or east):
                    continue
                first = COL0 - RIM + b + 8 * blk
                cells = padded[grp, r, first : first + 8]
                if part == "rim" and inner:
                    keep = lane < RIM - b if west else lane >= 8 + RIM - b
                    cells = jnp.where(keep, cells, 0.0)
                for a in range(KERNEL):
                    row = r - a
                    if 0 <= row < edge:
                        term = cells * weights[a]
                        acc[row] = term if acc[row] is None else acc[row] + term
        for row in range(edge):
            emit(blk, row, acc[row])


def kernel_grad_group(padded, grad, sums, grp, edge):
    for b in range(KERNEL):
        acc = [None] * KERNEL
        for blk in range(edge // 8):
            rows = [grad[grp, RIM + i, COL0 + 8 * blk : COL0 + 8 * blk + 8] for i in range(edge)]
            for r in range(edge + 2 * RIM):
                first = COL0 - RIM + b + 8 * blk
                cells = padded[0, grp, r, first : first + 8]
                for a in range(KERNEL):
                    if 0 <= r - a < edge:
                        term = rows[r - a] * cells
                        acc[a] = term if acc[a] is None else acc[a] + term
        for a in range(KERNEL):
            sums[grp, a * KERNEL + b] += acc[a]


def pack_body(slot_ref, side_sends, corner_sends, field, send, cells, side, corner, *, edge):
    slots = field.shape[0]
    own = 4 * slots
    area = edge * edge
    for s in range(slots):
        factor = live_factor(slot_ref, s)
        for grp in range(cells.shape[0]):
            for i in list(range(edge)):
                row = field[s, i, :, grp * LANES : (grp + 1) * LANES].astype(F32)
                first = s * area + i * edge
                cells[grp, first : first + edge] = row * factor
    side[own] = jnp.zeros(side.shape[1:], F32)
    corner[...] = jnp.zeros_like(corner)
    own_records(cells, side, corner, 0, edge, slots)
    send_records(send, side, corner, side_sends, corner_sends, own)


def own_body(slot_ref, field, kernel_ref, mixed, padded, taps, *, edge):
    s = pl.program_id(0)
    groups = padded.shape[0]

    @pl.when(s == 0)
    def _():
        padded[...] = jnp.zeros_like(padded)
        spread_taps(taps, kernel_ref)

    factor = live_factor(slot_ref, s)
    for grp in range(groups):
        for i in range(edge):
            row = field[0, i, :, grp * LANES : (grp + 1) * LANES].astype(F32)
            padded[grp, RIM + i, COL0 : COL0 + edge] = row * factor

    def one_group(grp, carry):
        def emit(blk, row, total):
            mixed[0, grp, row, 8 * blk : 8 * blk + 8] = total

        conv_group(padded, taps, grp, edge, "own", False, emit)
        return carry

    lax.fori_loop(0, groups, one_group, 0)


def forward_body(
    slot_ref,
    side_sources,
    corner_sources,
    recv,
    field,
    mixed_own,
    cotangent,
    kernel_ref,
    expand,
    reduce,
    out,
    padded_out,
    unit_out,
    scale_out,
    slope_out,
    reduce_out,
    side,
    corner,
    cells,
    taps,
    mixed,
    reduce_sum,
    *,
    edge,
    cap,
):
    s = pl.program_id(0)
    slots = pl.num_programs(0)
    groups = taps.shape[0]
    area = edge * edge
    n_slots = field.shape[0]
    base = recv.shape[0] * cap
    zero_at = base + 4 * n_slots
    hidden = expand.shape[1]

    @pl.when(s == 0)
    def _():
        for t in range(n_slots):
            factor = live_factor(slot_ref, t)
            for grp in range(groups):
                for i in range(edge):
                    row = field[t, i, :, grp * LANES : (grp + 1) * LANES].astype(F32)
                    first = t * area + i * edge
                    cells[grp, first : first + edge] = row * factor
        side[zero_at] = jnp.zeros(side.shape[1:], F32)
        corner[zero_at] = jnp.zeros(corner.shape[1:], F32)
        received_records(recv, side, corner, cap)
        own_records(cells, side, corner, base, edge, n_slots)
        spread_taps(taps, kernel_ref)
        reduce_sum[...] = jnp.zeros_like(reduce_sum)

    padded = padded_out.at[0]
    for grp in range(groups):
        for i in range(edge):
            first = pl.multiple_of(s * area + i * edge, 8)
            padded[grp, RIM + i, COL0 : COL0 + edge] = cells[grp, pl.ds(first, edge)]
    place_rim(padded, side, corner, side_sources, corner_sources, s, zero_at, edge)

    def one_group(grp, carry):
        def emit(blk, row, total):
            own = mixed_own[0, grp, row, 8 * blk : 8 * blk + 8]
            first = row * edge + 8 * blk
            mixed[grp, first : first + 8] = own if total is None else own + total

        conv_group(padded, taps, grp, edge, "rim", False, emit)
        return carry

    lax.fori_loop(0, groups, one_group, 0)

    channels = groups * LANES
    parts = [mixed[grp] for grp in range(groups)]
    mean = sum(jnp.sum(part, axis=1, keepdims=True) for part in parts) * (1.0 / channels)
    parts = [part - mean for part in parts]
    var = sum(jnp.sum(part * part, axis=1, keepdims=True) for part in parts) * (1.0 / channels)
    scale = lax.rsqrt(var + LN_EPS)
    unit = jnp.concatenate([part * scale for part in parts], axis=1)
    unit_out[...] = unit
    scale_out[...] = scale
    normed = unit.astype(BF16)
    cot = cotangent[...]
    update = None
    for n in range(0, hidden, 256):
        pre = mxu(normed, expand[:, n : n + 256], 1, 0)
        act, slope = gelu_parts(pre)
        act = act.astype(BF16)
        slope_out[:, n : n + 256] = slope.astype(BF16)
        term = mxu(act, reduce[n : n + 256], 1, 0)
        update = term if update is None else update + term
        reduce_sum[:, n : n + 256] += mxu(cot, act, 0, 0)
    factor = live_factor(slot_ref, s)
    for grp in range(groups):
        lanes = slice(grp * LANES, (grp + 1) * LANES)
        first = pl.multiple_of(s * area, 8)
        total = cells[grp, pl.ds(first, area)] + update[:, lanes]
        out[:, lanes] = (total * factor).astype(BF16)

    @pl.when(s == slots - 1)
    def _():
        reduce_out[...] = jnp.transpose(reduce_sum[...]).astype(BF16)


def backward_body(
    slot_ref,
    side_sends,
    corner_sends,
    cotangent,
    unit_ref,
    scale_ref,
    slope_ref,
    expand,
    reduce,
    grad_out,
    expand_out,
    send,
    expand_sum,
    cells,
    side,
    corner,
    *,
    edge,
):
    s = pl.program_id(0)
    slots = pl.num_programs(0)
    groups = cells.shape[0]
    area = edge * edge
    hidden = expand.shape[1]

    @pl.when(s == 0)
    def _():
        expand_sum[...] = jnp.zeros_like(expand_sum)

    factor = live_factor(slot_ref, s)
    cot = (cotangent[...].astype(F32) * factor).astype(BF16)
    unit = unit_ref[...]
    normed = unit.astype(BF16)
    grad_norm = None
    for n in range(0, hidden, 256):
        grad_act = mxu(cot, reduce[n : n + 256], 1, 1)
        grad_pre = (grad_act * slope_ref[:, n : n + 256].astype(F32)).astype(BF16)
        expand_sum[:, n : n + 256] += mxu(normed, grad_pre, 0, 0)
        term = mxu(grad_pre, expand[:, n : n + 256], 1, 1)
        grad_norm = term if grad_norm is None else grad_norm + term
    channels = groups * LANES
    mean = jnp.sum(grad_norm, axis=1, keepdims=True) * (1.0 / channels)
    along = jnp.sum(grad_norm * unit, axis=1, keepdims=True) * (1.0 / channels)
    grad = (scale_ref[...] * (grad_norm - mean - unit * along)).astype(BF16)
    grad_out[...] = grad
    for grp in range(groups):
        first = pl.multiple_of(s * area, 8)
        cells[grp, pl.ds(first, area)] = grad[:, grp * LANES : (grp + 1) * LANES].astype(F32)

    @pl.when(s == slots - 1)
    def _():
        expand_out[...] = expand_sum[...].astype(BF16)
        n_slots = cells.shape[1] // area
        own = 4 * n_slots
        side[own] = jnp.zeros(side.shape[1:], F32)
        corner[...] = jnp.zeros_like(corner)
        own_records(cells, side, corner, 0, edge, n_slots)
        send_records(send, side, corner, side_sends, corner_sends, own)


def middle_body(padded_field, grad_ref, kernel_ref, spread, kernel_out, padded, taps, sums, *, edge):
    s = pl.program_id(0)
    groups = padded.shape[0]

    @pl.when(s == 0)
    def _():
        padded[...] = jnp.zeros_like(padded)
        spread_taps(taps, kernel_ref)
        sums[...] = jnp.zeros_like(sums)

    for grp in range(groups):
        for i in range(edge):
            row = grad_ref[i * edge : (i + 1) * edge, grp * LANES : (grp + 1) * LANES]
            padded[grp, RIM + i, COL0 : COL0 + edge] = row.astype(F32)

    def one_group(grp, carry):
        kernel_grad_group(padded_field, padded, sums, grp, edge)

        def emit(blk, row, total):
            spread[0, grp, row, 8 * blk : 8 * blk + 8] = total

        conv_group(padded, taps, grp, edge, "own", True, emit)
        return carry

    lax.fori_loop(0, groups, one_group, 0)

    @pl.when(s == pl.num_programs(0) - 1)
    def _():
        for grp in range(groups):
            lanes = slice(grp * LANES, (grp + 1) * LANES)
            kernel_out[:, lanes] = jnp.sum(sums[grp], axis=1)


def final_body(
    slot_ref,
    side_sources,
    corner_sources,
    recv,
    grad_ref,
    spread_own,
    cotangent,
    kernel_ref,
    out,
    side,
    corner,
    cells,
    padded,
    taps,
    *,
    edge,
    cap,
):
    s = pl.program_id(0)
    groups = taps.shape[0]
    area = edge * edge
    n_slots = grad_ref.shape[0] // area
    base = recv.shape[0] * cap
    zero_at = base + 4 * n_slots

    @pl.when(s == 0)
    def _():
        for grp in range(groups):
            cells[grp] = grad_ref[:, grp * LANES : (grp + 1) * LANES].astype(F32)
        side[zero_at] = jnp.zeros(side.shape[1:], F32)
        corner[zero_at] = jnp.zeros(corner.shape[1:], F32)
        received_records(recv, side, corner, cap)
        own_records(cells, side, corner, base, edge, n_slots)
        spread_taps(taps, kernel_ref)
        padded[...] = jnp.zeros_like(padded)

    place_rim(padded, side, corner, side_sources, corner_sources, s, zero_at, edge)
    factor = live_factor(slot_ref, s)
    for grp in range(groups):

        def emit(blk, row, total):
            cells_at = slice(8 * blk, 8 * blk + 8)
            own = spread_own[0, grp, row, cells_at]
            both = own if total is None else own + total
            lanes = slice(grp * LANES, (grp + 1) * LANES)
            first = row * edge + 8 * blk
            cot = cotangent[first : first + 8, lanes].astype(F32)
            out[first : first + 8, lanes] = ((cot + both) * factor).astype(BF16)

        conv_group(padded, taps, grp, edge, "rim", True, emit)


def call(body, name, grid, ins, outs, scratch, flops=0, moved=0, prefetch=0):
    in_specs = []
    for array, block, index in ins:
        if block is None:
            in_specs.append(pl.BlockSpec(memory_space=pltpu.SMEM))
        else:
            in_specs.append(pl.BlockSpec(block, index))
    return pl.pallas_call(
        body,
        name=name,
        grid=grid,
        in_specs=in_specs,
        out_specs=[pl.BlockSpec(block, index) for _, _, block, index in outs],
        out_shape=[jax.ShapeDtypeStruct(shape, dtype) for shape, dtype, _, _ in outs],
        scratch_shapes=scratch,
        compiler_params=pltpu.CompilerParams(vmem_limit_bytes=VMEM_LIMIT),
        cost_estimate=pl.CostEstimate(flops=flops, bytes_accessed=moved, transcendentals=0),
    )(*[array for array, _, _ in ins])


def whole(array):
    rank = array.ndim
    return (array, array.shape, lambda s: (0,) * rank)


def swap(blocks, axis):
    return lax.all_to_all(blocks, axis, split_axis=0, concat_axis=0, tiled=True)


def sum_everywhere(part, basins, tiles):
    rows, columns = part.shape
    blocks = swap(part.reshape(basins, rows // basins, columns), "basin")
    mine = jnp.sum(blocks.astype(F32), axis=0).astype(BF16)
    blocks = swap(mine.reshape(tiles, rows // basins // tiles, columns), "tile")
    mine = jnp.sum(blocks.astype(F32), axis=0).astype(BF16)
    blocks = swap(jnp.broadcast_to(mine[None], (tiles,) + mine.shape), "tile")
    mine = blocks.reshape(rows // basins, columns)
    blocks = swap(jnp.broadcast_to(mine[None], (basins,) + mine.shape), "basin")
    return blocks.reshape(rows, columns)


def sum_small(part, basins, tiles):
    for axis, size in (("basin", basins), ("tile", tiles)):
        blocks = swap(jnp.broadcast_to(part[None], (size,) + part.shape), axis)
        part = jnp.sum(blocks, axis=0)
    return part


def on_device(
    ocean_fields,
    slot_tiles,
    side_sources,
    corner_sources,
    side_sends,
    corner_sends,
    depth_kernel,
    expand_weight,
    reduce_weight,
    field_cotangent,
):
    slots, edge, _, channels = ocean_fields.shape
    hidden = expand_weight.shape[1]
    tiles = lax.axis_size("tile")
    basins = lax.axis_size("basin")
    cap = side_sends.shape[2]
    groups = channels // LANES
    area = edge * edge
    cells = slots * area
    n_side = RIM * edge
    n_corner = 16
    send_rows = cap * (n_side + n_corner)
    table = tiles * cap + 4 * slots + 1
    wide = edge + 2 * COL0
    tall = edge + 2 * RIM

    side_sends = side_sends.reshape(-1)
    corner_sends = corner_sends.reshape(-1)
    side_sources = side_sources.reshape(-1)
    corner_sources = corner_sources.reshape(-1)
    cot_rows = field_cotangent.reshape(cells, channels)
    scalar = lambda array: (array, None, None)
    by_slot = lambda array, width: (array, (area, width), lambda s: (s, 0))
    taps = pltpu.VMEM((groups, TAPS, 8, LANES), F32)
    cell_scratch = pltpu.VMEM((groups, cells, LANES), F32)
    padded_scratch = pltpu.VMEM((groups, tall, wide, LANES), F32)
    own_side = pltpu.VMEM((4 * slots + 1, groups, n_side, LANES), F32)
    own_corner = pltpu.VMEM((4 * slots + 1, groups, n_corner, LANES), F32)
    all_side = pltpu.VMEM((table, groups, n_side, LANES), F32)
    all_corner = pltpu.VMEM((table, groups, n_corner, LANES), F32)
    send_out = ((tiles, send_rows, channels), BF16, (tiles, send_rows, channels), lambda s: (0, 0, 0))
    tile_block = (1, groups, edge, edge, LANES)
    tile_out = ((slots,) + tile_block[1:], F32, tile_block, lambda s: (s, 0, 0, 0, 0))
    mlp_flops = 6 * cells * channels * hidden
    field_bytes = cells * channels * 4

    (send,) = call(
        functools.partial(pack_body, edge=edge),
        "pack_field",
        (1,),
        [scalar(slot_tiles), scalar(side_sends), scalar(corner_sends), whole(ocean_fields)],
        [send_out],
        [cell_scratch, own_side, own_corner],
        moved=field_bytes,
    )
    recv = swap(send, "tile")
    (mixed_own,) = call(
        functools.partial(own_body, edge=edge),
        "mix_own",
        (slots,),
        [
            scalar(slot_tiles),
            (ocean_fields, (1, edge, edge, channels), lambda s: (s, 0, 0, 0)),
            whole(depth_kernel),
        ],
        [tile_out],
        [padded_scratch, taps],
        flops=mlp_flops,
        moved=2 * field_bytes,
    )
    next_rows, padded, unit, scale, slope, reduce_part = call(
        functools.partial(forward_body, edge=edge, cap=cap),
        "forward",
        (slots,),
        [
            scalar(slot_tiles),
            scalar(side_sources),
            scalar(corner_sources),
            whole(recv),
            whole(ocean_fields),
            (mixed_own, tile_block, lambda s: (s, 0, 0, 0, 0)),
            by_slot(cot_rows, channels),
            whole(depth_kernel),
            whole(expand_weight),
            whole(reduce_weight),
        ],
        [
            ((cells, channels), BF16, (area, channels), lambda s: (s, 0)),
            (
                (slots, groups, tall, wide, LANES),
                F32,
                (1, groups, tall, wide, LANES),
                lambda s: (s, 0, 0, 0, 0),
            ),
            ((cells, channels), F32, (area, channels), lambda s: (s, 0)),
            ((cells, 1), F32, (area, 1), lambda s: (s, 0)),
            ((cells, hidden), BF16, (area, hidden), lambda s: (s, 0)),
            ((hidden, channels), BF16, (hidden, channels), lambda s: (0, 0)),
        ],
        [
            all_side,
            all_corner,
            cell_scratch,
            taps,
            pltpu.VMEM((groups, area, LANES), F32),
            pltpu.VMEM((channels, hidden), F32),
        ],
        flops=mlp_flops,
        moved=6 * field_bytes,
    )
    reduce_total = sum_everywhere(reduce_part, basins, tiles)
    grad_rows, expand_part, send = call(
        functools.partial(backward_body, edge=edge),
        "backward",
        (slots,),
        [
            scalar(slot_tiles),
            scalar(side_sends),
            scalar(corner_sends),
            by_slot(cot_rows, channels),
            by_slot(unit, channels),
            (scale, (area, 1), lambda s: (s, 0)),
            by_slot(slope, hidden),
            whole(expand_weight),
            whole(reduce_weight),
        ],
        [
            ((cells, channels), BF16, (area, channels), lambda s: (s, 0)),
            ((channels, hidden), BF16, (channels, hidden), lambda s: (0, 0)),
            send_out,
        ],
        [pltpu.VMEM((channels, hidden), F32), cell_scratch, own_side, own_corner],
        flops=mlp_flops,
        moved=5 * field_bytes,
    )
    recv = swap(send, "tile")
    expand_total = sum_everywhere(expand_part, basins, tiles)
    spread_own, kernel_part = call(
        functools.partial(middle_body, edge=edge),
        "middle",
        (slots,),
        [
            (padded, (1, groups, tall, wide, LANES), lambda s: (s, 0, 0, 0, 0)),
            by_slot(grad_rows, channels),
            whole(depth_kernel),
        ],
        [tile_out, ((TAPS, channels), F32, (TAPS, channels), lambda s: (0, 0))],
        [padded_scratch, taps, taps],
        flops=2 * mlp_flops,
        moved=4 * field_bytes,
    )
    kernel_total = sum_small(kernel_part, basins, tiles)
    (grad_field,) = call(
        functools.partial(final_body, edge=edge, cap=cap),
        "final",
        (slots,),
        [
            scalar(slot_tiles),
            scalar(side_sources),
            scalar(corner_sources),
            whole(recv),
            whole(grad_rows),
            (spread_own, tile_block, lambda s: (s, 0, 0, 0, 0)),
            by_slot(cot_rows, channels),
            whole(depth_kernel),
        ],
        [((cells, channels), BF16, (area, channels), lambda s: (s, 0))],
        [all_side, all_corner, cell_scratch, padded_scratch, taps],
        flops=mlp_flops // 2,
        moved=3 * field_bytes,
    )
    factor = 1.0 / math.sqrt(basins * tiles * cells)
    shape = ocean_fields.shape
    return (
        next_rows.reshape(shape),
        grad_field.reshape(shape),
        kernel_total * factor,
        expand_total.astype(F32) * factor,
        reduce_total.astype(F32) * factor,
    )


def solution(mesh):
    split = ("basin", "tile")
    field = P(split, None, None, None)
    table = P(split, None, None)
    pair = P(split, None)
    return jax.shard_map(
        on_device,
        mesh=mesh,
        in_specs=(field, P(split), pair, pair, table, table, P(), P(), P(), field),
        out_specs=(field, field, P(), P(), P()),
        check_vma=False,
    )
```

time: 287 us -> 232 us (0.81)
  other arithmetic: 88.7 us -> 4.39 us
  Pallas kernels: 0 us -> 78.2 us
  waiting for transfers between devices: 83.1 us -> 57.3 us
  matrix products: 19 us -> 0 us
  between operations: 16.1 us -> 0.76 us
  blocking collectives: 41.6 us -> 54.1 us
  local copies, waits for them, and re-layouts: 18.1 us -> 8.08 us
  starting transfers between devices: 19.1 us -> 28.2 us
    pallas_call x0 -> x6, Pallas kernels: none -> 78.2 us  [call(): pl.pallas_call(body, name=name, grid=grid, in_specs=in_specs, out_specs=[...]
    psum x1 -> x0, waiting for transfers between devices: 63.4 us -> none  [on_device(): lax.psum((kernel_local, expand_local, reduce_local), ('basin', 'tile'))]
    all_to_all x0 -> x5, blocking collectives: none -> 54.1 us  [swap(): return lax.all_to_all(blocks, axis, split_axis=0, concat_axis=0, tiled=True)]
    psum x1 -> x0, blocking collectives: 41.6 us -> none  [on_device(): lax.psum((kernel_local, expand_local, reduce_local), ('basin', 'tile'))]
    all_to_all x4 -> x7, waiting for transfers between devices: 19.6 us -> 57.3 us  [swap(): return lax.all_to_all(blocks, axis, split_axis=0, concat_axis=0, tiled=True)]
    reduce_sum x6, other arithmetic: 38.6 us -> 1.59 us  [the longest x4 1.54 us: sum_everywhere(): mine = jnp.sum(blocks.astype(F32), axis=0).astype(BF16)]
    select_n x15 -> x0, other arithmetic: 28.9 us -> none  [the longest x1 21.3 us: on_device(): jnp.where(live_mask, (cotangent.astype(jnp.float32) + spread).astype(jnp....]
    dot_general x6 -> x0, matrix products: 19 us -> none  [the longest x1 4.72 us: on_device(): jnp.einsum('rc,rf->cf', normed, grad_pre, preferred_element_type=jnp.floa...]
  transfers between devices with their start and end apart: 5 -> 7, of which waited for: 4 -> 7; matrix products, arithmetic and copies ran while one was open for 16% -> 2% of each run, Pallas kernels for 0% -> 5%
where the time goes in v1:
time: 232 us; the launch traced here: 231 us
  Pallas kernels  78.2 us (34%)
  waiting for transfers between devices  57.3 us (25%)
  blocking collectives  54.1 us (23%)
  starting transfers between devices  28.2 us (12%)
  local copies, waits for them, and re-layouts  8.08 us (3%)
  other arithmetic  4.39 us (2%)
    pallas_call x6, Pallas kernels, call(): pl.pallas_call(body, name=name, grid=grid, in_specs=in_specs, out_specs=[...  78.2 us
    all_to_all x7, waiting for transfers between devices, swap(): return lax.all_to_all(blocks, axis, split_axis=0, concat_axis=0, tiled=True)  57.3 us
    all_to_all x5, blocking collectives, swap(): return lax.all_to_all(blocks, axis, split_axis=0, concat_axis=0, tiled=True)  54.1 us
    all_to_all x7, starting transfers between devices, swap(): return lax.all_to_all(blocks, axis, split_axis=0, concat_axis=0, tiled=True)  28.2 us
  transfers between devices with their start and end apart: 7, of which 7 were waited for; matrix products, arithmetic and copies ran while one was open for 2% of the time, Pallas kernels for 5%

profile of v1, /device:TPU:0, one launch (start us, length us, event | category | flops | bytes accessed | tf_op | source)
XLA Modules:
  0.0 231.0 jit_solution(7577246951308769257)
XLA Ops:
  0.6 0.8 copy.21
  1.4 0.6 reshape.59.side_sends
  2.0 0.8 copy.22
  2.7 0.7 reshape.60.corner_sends
  3.4 2.6 %pack_field.1 = bf16[8,176,256]{2,1,0:T(8,128)(2,1)} custom-call(s32[4]{0:T(128)} %slot_ref.9, s32[16]{0:T(128)} %reshape.59.side_sends, s32[16]{0:T(128)} %reshape.60.corner_sends, bf16[4,24,24,256]{3,2,1,0:T(8,128)(2,1)} %field.5), custom_call_target="tpu_custom_call" | custom-call | bytes 2359296 | tf_op jit(solution)/shard_map/pack_field/pallas_call | solution.py:473
  6.0 0.0 copy-start.3
  6.0 0.0 copy-start.4
  6.0 7.4 %all-to-all-start = ((bf16[8,176,256]{2,1,0:T(8,128)(2,1)}), bf16[8,176,256]{2,1,0:T(8,128)(2,1)S(1)}, u32[]{:S(2)}, u32[]{:S(2)}) async-start(bf16[8,176,256]{2,1,0:T(8,128)(2,1)} %pack_field.1), calls=%async_computation | async-start | bytes 1441792 | tf_op jit(solution)/shard_map/all_to_all | solution.py:492
  13.5 0.0 copy-done.3
  13.5 0.7 reshape.57.side_sources
  14.1 0.0 copy-done.4
  14.1 0.6 reshape.58.corner_sources
  14.8 12.2 %mix_own.1.mixed_own = f32[4,2,24,24,128]{4,3,2,1,0:T(8,128)} custom-call(s32[4]{0:T(128)} %slot_ref.9, bf16[4,24,24,256]{3,2,1,0:T(8,128)(2,1)} %field.5, bf16[49,256]{1,0:T(8,128)(2,1)} %kernel_ref.7), custom_call_target="tpu_custom_call" | custom-call | flops 3623878656 | bytes 4718592 | tf_op jit(solution)/shard_map/mix_own/pallas_call | solution.py:473
  27.0 5.2 %all-to-all-done.recv = bf16[8,176,256]{2,1,0:T(8,128)(2,1)S(1)} async-done(((bf16[8,176,256]{2,1,0:T(8,128)(2,1)}), bf16[8,176,256]{2,1,0:T(8,128)(2,1)S(1)}, u32[]{:S(2)}, u32[]{:S(2)}) %all-to-all-start) | async-done | bytes 720928 | tf_op jit(solution)/shard_map/all_to_all | solution.py:492
  32.2 0.0 copy-start.1
  32.2 0.9 copy-done.1
  33.0 17.1 %forward.1 = (bf16[2304,256]{1,0:T(8,128)(2,1)}, f32[4,2,30,40,128]{4,3,2,1,0:T(8,128)}, f32[2304,256]{1,0:T(8,128)}, f32[2304,1]{1,0:T(8,128)}, bf16[2304,1024]{1,0:T(8,128)(2,1)}, /*index=5*/bf16[1024,256]{1,0:T(8,128)(2,1)}) custom-call(s32[4]{0:T(128)} %slot_ref.9, s32[16]{0:T(128)} %reshape.57.side_sources, s32[16]{0:T(128)} %reshape.58.corner_sources, ...), custom_call_target="tpu_custom_call" | custom-call | flops 3623878656 | bytes 14155776 | tf_op jit(solution)/shard_map/forward/pallas_call | solution.py:473
  50.1 11.7 %backward.1 = (bf16[2304,256]{1,0:T(8,128)(2,1)}, bf16[256,1024]{1,0:T(8,128)(2,1)}, bf16[8,176,256]{2,1,0:T(8,128)(2,1)}) custom-call(s32[4]{0:T(128)} %slot_ref.9, s32[16]{0:T(128)} %reshape.59.side_sends, s32[16]{0:T(128)} %reshape.60.corner_sends, bf16[2304,256]{1,0:T(8,128)(2,1)} %bitcast.17, f32[2304,256]{1,0:T(8,128)} %get-tuple-element.17.unit_ref, ...), custom_call_target="tpu_custom_call" | custom-call | flops 3623878656 | bytes 11796480 | tf_op jit(solution)/shard_map/backward/pallas_call | solution.py:473
  61.9 0.0 copy-start.2
  61.9 27.6 %middle.1 = (f32[4,2,24,24,128]{4,3,2,1,0:T(8,128)}, f32[49,256]{1,0:T(8,128)}) custom-call(f32[4,2,30,40,128]{4,3,2,1,0:T(8,128)} %get-tuple-element.22.padded_field, bf16[2304,256]{1,0:T(8,128)(2,1)} %get-tuple-element.21.grad_ref, bf16[49,256]{1,0:T(8,128)(2,1)} %kernel_ref.7), custom_call_target="tpu_custom_call" | custom-call | flops 7247757312 | bytes 9437184 | tf_op jit(solution)/shard_map/middle/pallas_call | solution.py:473
  89.5 0.8 broadcast_in_dim.16
  90.3 8.2 %all_to_all.60 = f32[4,49,256]{2,1,0:T(8,128)S(1)} all-to-all(f32[4,49,256]{2,1,0:T(8,128)S(1)} %broadcast_in_dim.16), channel_id=1, replica_groups=mesh['basin'=4,'tile'=8] {'basin'}, dimensions={0} | all-to-all | bytes 401408 | tf_op jit(solution)/shard_map/all_to_all | solution.py:492
  98.5 0.0 copy-done.2
  98.5 11.2 %all_to_all.61 = bf16[4,256,256]{2,1,0:T(8,128)(2,1)S(1)} all-to-all(bf16[4,256,256]{2,1,0:T(8,128)(2,1)S(1)} %bitcast.15), channel_id=1, replica_groups=mesh['basin'=4,'tile'=8] {'basin'}, dimensions={0} | all-to-all | bytes 1048576 | tf_op jit(solution)/shard_map/all_to_all | solution.py:492
  109.7 3.5 %all-to-all-start.4 = ((bf16[4,64,1024]{2,1,0:T(8,128)(2,1)}), bf16[4,64,1024]{2,1,0:T(8,128)(2,1)S(1)}, u32[]{:S(2)}, u32[]{:S(2)}) async-start(bf16[4,64,1024]{2,1,0:T(8,128)(2,1)} %bitcast.3), calls=%async_computation.4 | async-start | bytes 1048576 | tf_op jit(solution)/shard_map/all_to_all | solution.py:492
  113.2 0.7 reduce_sum.70
  114.0 8.0 %all-to-all-done.4 = bf16[4,64,1024]{2,1,0:T(8,128)(2,1)S(1)} async-done(((bf16[4,64,1024]{2,1,0:T(8,128)(2,1)}), bf16[4,64,1024]{2,1,0:T(8,128)(2,1)S(1)}, u32[]{:S(2)}, u32[]{:S(2)}) %all-to-all-start.4) | async-done | bytes 524320 | tf_op jit(solution)/shard_map/all_to_all | solution.py:492
  122.0 3.6 %all-to-all-start.9 = ((bf16[8,32,256]{2,1,0:T(8,128)(2,1)}), bf16[8,32,256]{2,1,0:T(8,128)(2,1)S(1)}, u32[]{:S(2)}, u32[]{:S(2)}) async-start(bf16[8,32,256]{2,1,0:T(8,128)(2,1)} %bitcast.8), calls=%async_computation.9 | async-start | bytes 262144 | tf_op jit(solution)/shard_map/all_to_all | solution.py:492
  125.6 0.7 reduce_sum.68
  126.4 6.6 %all-to-all-done.9 = bf16[8,32,256]{2,1,0:T(8,128)(2,1)S(1)} async-done(((bf16[8,32,256]{2,1,0:T(8,128)(2,1)}), bf16[8,32,256]{2,1,0:T(8,128)(2,1)S(1)}, u32[]{:S(2)}, u32[]{:S(2)}) %all-to-all-start.9) | async-done | bytes 131104 | tf_op jit(solution)/shard_map/all_to_all | solution.py:492
  133.0 3.4 %all-to-all-start.5 = ((bf16[8,8,1024]{2,1,0:T(8,128)(2,1)}), bf16[8,8,1024]{2,1,0:T(8,128)(2,1)S(1)}, u32[]{:S(2)}, u32[]{:S(2)}) async-start(bf16[8,8,1024]{2,1,0:T(8,128)(2,1)} %bitcast.4), calls=%async_computation.5 | async-start | bytes 262144 | tf_op jit(solution)/shard_map/all_to_all | solution.py:492
  136.4 7.2 %all-to-all-done.5 = bf16[8,8,1024]{2,1,0:T(8,128)(2,1)S(1)} async-done(((bf16[8,8,1024]{2,1,0:T(8,128)(2,1)}), bf16[8,8,1024]{2,1,0:T(8,128)(2,1)S(1)}, u32[]{:S(2)}, u32[]{:S(2)}) %all-to-all-start.5) | async-done | bytes 131104 | tf_op jit(solution)/shard_map/all_to_all | solution.py:492
  143.6 0.7 broadcast_in_dim.21
  144.3 3.4 %all-to-all-start.10 = ((bf16[8,32,256]{2,1,0:T(8,128)(2,1)}), bf16[8,32,256]{2,1,0:T(8,128)(2,1)S(1)}, u32[]{:S(2)}, u32[]{:S(2)}) async-start(bf16[8,32,256]{2,1,0:T(8,128)(2,1)} %broadcast_in_dim.21), calls=%async_computation.10 | async-start | bytes 262144 | tf_op jit(solution)/shard_map/all_to_all | solution.py:492
  147.7 7.2 %all-to-all-done.10 = bf16[8,32,256]{2,1,0:T(8,128)(2,1)S(1)} async-done(((bf16[8,32,256]{2,1,0:T(8,128)(2,1)}), bf16[8,32,256]{2,1,0:T(8,128)(2,1)S(1)}, u32[]{:S(2)}, u32[]{:S(2)}) %all-to-all-start.10) | async-done | bytes 131104 | tf_op jit(solution)/shard_map/all_to_all | solution.py:492
  154.9 0.7 broadcast_in_dim.18
  155.6 3.4 %all-to-all-start.6 = ((bf16[8,8,1024]{2,1,0:T(8,128)(2,1)}), bf16[8,8,1024]{2,1,0:T(8,128)(2,1)S(1)}, u32[]{:S(2)}, u32[]{:S(2)}) async-start(bf16[8,8,1024]{2,1,0:T(8,128)(2,1)} %broadcast_in_dim.18), calls=%async_computation.6 | async-start | bytes 262144 | tf_op jit(solution)/shard_map/all_to_all | solution.py:492
  159.0 7.3 %all-to-all-done.6 = bf16[8,8,1024]{2,1,0:T(8,128)(2,1)S(1)} async-done(((bf16[8,8,1024]{2,1,0:T(8,128)(2,1)}), bf16[8,8,1024]{2,1,0:T(8,128)(2,1)S(1)}, u32[]{:S(2)}, u32[]{:S(2)}) %all-to-all-start.6) | async-done | bytes 131104 | tf_op jit(solution)/shard_map/all_to_all | solution.py:492
  166.3 12.3 %all_to_all.62 = f32[8,49,256]{2,1,0:T(8,128)S(1)} all-to-all(f32[8,49,256]{2,1,0:T(8,128)S(1)} %broadcast_in_dim.17), channel_id=1, replica_groups=mesh['basin'=4,'tile'=8] {'tile'}, dimensions={0} | all-to-all | bytes 802816 | tf_op jit(solution)/shard_map/all_to_all | solution.py:492
  178.7 11.2 %all_to_all.63 = bf16[4,256,256]{2,1,0:T(8,128)(2,1)S(1)} all-to-all(bf16[4,256,256]{2,1,0:T(8,128)(2,1)S(1)} %broadcast_in_dim.45), channel_id=1, replica_groups=mesh['basin'=4,'tile'=8] {'basin'}, dimensions={0} | all-to-all | bytes 1048576 | tf_op jit(solution)/shard_map/all_to_all | solution.py:492
  189.9 11.2 %all_to_all.64 = bf16[4,64,1024]{2,1,0:T(8,128)(2,1)S(1)} all-to-all(bf16[4,64,1024]{2,1,0:T(8,128)(2,1)S(1)} %broadcast_in_dim.20), channel_id=1, replica_groups=mesh['basin'=4,'tile'=8] {'basin'}, dimensions={0} | all-to-all | bytes 1048576 | tf_op jit(solution)/shard_map/all_to_all | solution.py:492
  201.1 3.5 %all-to-all-start.1 = ((bf16[8,176,256]{2,1,0:T(8,128)(2,1)}), bf16[8,176,256]{2,1,0:T(8,128)(2,1)S(1)}, u32[]{:S(2)}, u32[]{:S(2)}) async-start(bf16[8,176,256]{2,1,0:T(8,128)(2,1)} %get-tuple-element.20), calls=%async_computation.1 | async-start | bytes 1441792 | tf_op jit(solution)/shard_map/all_to_all | solution.py:492
  204.7 0.6 broadcast_multiply_fusion
  205.4 1.1 convert_multiply_fusion
  206.4 1.1 convert_multiply_fusion.1
  207.5 15.8 %all-to-all-done.1.recv = bf16[8,176,256]{2,1,0:T(8,128)(2,1)S(1)} async-done(((bf16[8,176,256]{2,1,0:T(8,128)(2,1)}), bf16[8,176,256]{2,1,0:T(8,128)(2,1)S(1)}, u32[]{:S(2)}, u32[]{:S(2)}) %all-to-all-start.1) | async-done | bytes 720928 | tf_op jit(solution)/shard_map/all_to_all | solution.py:492
  223.3 0.0 copy-start
  223.3 0.9 copy-done
  224.1 6.9 %final.1 = bf16[2304,256]{1,0:T(8,128)(2,1)} custom-call(s32[4]{0:T(128)} %slot_ref.9, s32[16]{0:T(128)} %reshape.57.side_sources, s32[16]{0:T(128)} %reshape.58.corner_sources, bf16[8,176,256]{2,1,0:T(8,128)(2,1)} %copy-done, bf16[2304,256]{1,0:T(8,128)(2,1)} %get-tuple-element.21.grad_ref, f32[4,2,24,24,128]{4,3,2,1,0:T(8,128)} %get-tuple-element.23.spread_own, ...), custom_call_target="tpu_custom_call" | custom-call | flops 1811939328 | bytes 7077888 | tf_op jit(solution)/shard_map/final/pallas_call | solution.py:473
  (7 shorter events, 0.2 us)
Async XLA Ops:
  6.0 7.4 %copy-start.3 = (s32[4,4]{1,0:T(4,128)S(1)}, s32[4,4]{1,0:T(4,128)}, u32[]{:S(2)}) copy-start(s32[4,4]{1,0:T(4,128)} %param.12) | copy-start | bytes 196
  6.0 8.1 %copy-start.4 = (s32[4,4]{1,0:T(4,128)S(1)}, s32[4,4]{1,0:T(4,128)}, u32[]{:S(2)}) copy-start(s32[4,4]{1,0:T(4,128)} %param.13) | copy-start | bytes 196
  6.0 26.2 %all-to-all-start = ((bf16[8,176,256]{2,1,0:T(8,128)(2,1)}), bf16[8,176,256]{2,1,0:T(8,128)(2,1)S(1)}, u32[]{:S(2)}, u32[]{:S(2)}) async-start(bf16[8,176,256]{2,1,0:T(8,128)(2,1)} %pack_field.1), calls=%async_computation | async-start | bytes 1441792 | tf_op jit(solution)/shard_map/all_to_all | solution.py:492
  32.2 0.9 copy-start.1
  61.9 36.7 %copy-start.2 = (bf16[1024,256]{1,0:T(8,128)(2,1)S(1)}, bf16[1024,256]{1,0:T(8,128)(2,1)}, u32[]{:S(2)}) copy-start(bf16[1024,256]{1,0:T(8,128)(2,1)} %get-tuple-element.26) | copy-start | bytes 1572868
  109.7 12.3 %all-to-all-start.4 = ((bf16[4,64,1024]{2,1,0:T(8,128)(2,1)}), bf16[4,64,1024]{2,1,0:T(8,128)(2,1)S(1)}, u32[]{:S(2)}, u32[]{:S(2)}) async-start(bf16[4,64,1024]{2,1,0:T(8,128)(2,1)} %bitcast.3), calls=%async_computation.4 | async-start | bytes 1048576 | tf_op jit(solution)/shard_map/all_to_all | solution.py:492
  122.0 11.0 %all-to-all-start.9 = ((bf16[8,32,256]{2,1,0:T(8,128)(2,1)}), bf16[8,32,256]{2,1,0:T(8,128)(2,1)S(1)}, u32[]{:S(2)}, u32[]{:S(2)}) async-start(bf16[8,32,256]{2,1,0:T(8,128)(2,1)} %bitcast.8), calls=%async_computation.9 | async-start | bytes 262144 | tf_op jit(solution)/shard_map/all_to_all | solution.py:492
  133.0 10.7 %all-to-all-start.5 = ((bf16[8,8,1024]{2,1,0:T(8,128)(2,1)}), bf16[8,8,1024]{2,1,0:T(8,128)(2,1)S(1)}, u32[]{:S(2)}, u32[]{:S(2)}) async-start(bf16[8,8,1024]{2,1,0:T(8,128)(2,1)} %bitcast.4), calls=%async_computation.5 | async-start | bytes 262144 | tf_op jit(solution)/shard_map/all_to_all | solution.py:492
  144.3 10.7 %all-to-all-start.10 = ((bf16[8,32,256]{2,1,0:T(8,128)(2,1)}), bf16[8,32,256]{2,1,0:T(8,128)(2,1)S(1)}, u32[]{:S(2)}, u32[]{:S(2)}) async-start(bf16[8,32,256]{2,1,0:T(8,128)(2,1)} %broadcast_in_dim.21), calls=%async_computation.10 | async-start | bytes 262144 | tf_op jit(solution)/shard_map/all_to_all | solution.py:492
  155.6 10.7 %all-to-all-start.6 = ((bf16[8,8,1024]{2,1,0:T(8,128)(2,1)}), bf16[8,8,1024]{2,1,0:T(8,128)(2,1)S(1)}, u32[]{:S(2)}, u32[]{:S(2)}) async-start(bf16[8,8,1024]{2,1,0:T(8,128)(2,1)} %broadcast_in_dim.18), calls=%async_computation.6 | async-start | bytes 262144 | tf_op jit(solution)/shard_map/all_to_all | solution.py:492
  201.1 22.1 %all-to-all-start.1 = ((bf16[8,176,256]{2,1,0:T(8,128)(2,1)}), bf16[8,176,256]{2,1,0:T(8,128)(2,1)S(1)}, u32[]{:S(2)}, u32[]{:S(2)}) async-start(bf16[8,176,256]{2,1,0:T(8,128)(2,1)} %get-tuple-element.20), calls=%async_computation.1 | async-start | bytes 1441792 | tf_op jit(solution)/shard_map/all_to_all | solution.py:492
  223.3 0.9 copy-start
